TPU v7x, 32 devices: a whole 2x2x4 slice. The times are simulated.
32 devices in a mesh: groups: 1, ctx: 32 (over z, y, x, core).
Axes of the slice: x: 2, y: 2, z: 4, core: 2. Of those that a mesh axis runs over, the one named last changes fastest.
Arguments:
- prefill_query: bfloat16 [1024, 32, 576], P('groups', 'ctx'), may hold values from -1000 to 1000
- prefill_latent: bfloat16 [1024, 576], P(('groups', 'ctx')), may hold values from -6 to 6
- decode_query: bfloat16 [2, 32, 576], P('groups'), may hold values from -1000 to 1000
- cache: bfloat16 [2, 16384, 576], P('groups', 'ctx'), may hold values from -6 to 6
- lengths: int32 [2], P('groups'), may hold values from 2049 to 16384
- page_table: int32 [64, 2], P('groups'), may hold values from 0 to 31, as said below
Outputs:
- prefill_out: bfloat16 [1024, 32, 512], P('groups', 'ctx')
- decode_out: bfloat16 [2, 32, 512], P('groups', 'ctx')
Inputs may be any that keep to these rules, and one draw needn't show every extreme that they name: `page_table`: row p names the device (column 0, below 32) and the pool slot (column 1, below 16) that take latent page p; no two rows name the same pair.
All inputs are finite; a program needn't handle non-finite values.
Results may differ from a plain program's by a relative error of at most 0.0049.
Values may be sent and summed in bfloat16 or wider, within the bound.
No kernel may reach another device: no remote copies, remote signals or barrier semaphores. Data moves between devices by JAX's collectives and lax.ppermute only.
A program may use at most 64 MiB of HBM per device.

v0:
```python
import jax
import jax.numpy as jnp
from jax import lax
from jax.sharding import PartitionSpec as P

D_LAT = 512
PAGE = 16
POOL = 16
REQ = 2
SCALE = 192.0 ** (-0.5)
NEG = -1e30


def attend_block(state_now, queries, shard_rows, first_row):
    run_max, run_sum, weighted = state_now
    length = shard_rows.shape[0]
    scores = (
        jnp.einsum("ihc,jc->ihj", queries, shard_rows, preferred_element_type=jnp.float32) * SCALE
    )
    row_index = jnp.arange(queries.shape[0], dtype=jnp.int32)
    key_index = first_row + jnp.arange(length, dtype=jnp.int32)
    allowed = (key_index[None, :] <= row_index[:, None])[:, None, :]
    masked = jnp.where(allowed, scores, NEG)
    new_max = jnp.maximum(run_max, jnp.max(masked, axis=2))
    weights = jnp.where(allowed, jnp.exp(scores - new_max[:, :, None]), 0.0)
    factor = jnp.exp(run_max - new_max)
    new_sum = run_sum * factor + jnp.sum(weights, axis=2)
    product = jnp.einsum(
        "ihj,jv->ihv",
        weights.astype(jnp.bfloat16),
        shard_rows[:, :D_LAT],
        preferred_element_type=jnp.float32,
    )
    return (new_max, new_sum, weighted * factor[:, :, None] + product)


def attend_blocks(state_now, queries, shard_rows, first_row):
    length = shard_rows.shape[0]
    block_rows = min(length, 512)
    starts = list(range(0, length, block_rows))
    for start in starts:
        stop = min(start + block_rows, length)
        state_now = attend_block(state_now, queries, shard_rows[start:stop], first_row + start)
    return state_now


def pick_rows(shard_rows, first_row, source_rows, pool_live):
    length = shard_rows.shape[0]
    local_rows = source_rows - first_row
    inside = (local_rows >= 0) & (local_rows < length) & pool_live
    taken = jnp.take(shard_rows, jnp.clip(local_rows, 0, length - 1), axis=0)
    return jnp.where(inside[:, None], taken, jnp.zeros_like(taken))


def shards(prefill_query, prefill_latent, decode_query, cache, lengths, page_table):
    device = lax.axis_index("ctx")
    span = prefill_query.shape[0]
    head_here = prefill_query.shape[1]
    width = prefill_latent.shape[1]
    page_count = page_table.shape[0]
    slot_index = jnp.arange(POOL, dtype=jnp.int32)
    chosen = (page_table[None, :, 0] == device) & (page_table[None, :, 1] == slot_index[:, None])
    slot_live = jnp.any(chosen, axis=1)
    slot_page = jnp.sum(
        jnp.where(chosen, jnp.arange(page_count, dtype=jnp.int32)[None, :], 0), axis=1
    )
    offsets = jnp.arange(PAGE, dtype=jnp.int32)
    source_rows = (slot_page[:, None] * PAGE + offsets[None, :]).reshape(-1)
    pool_live = jnp.repeat(slot_live, PAGE)
    pool_request = jnp.repeat((device * POOL + slot_index) % REQ, PAGE)
    initial = (
        jnp.full((span, head_here), NEG, jnp.float32),
        jnp.zeros((span, head_here), jnp.float32),
        jnp.zeros((span, head_here, D_LAT), jnp.float32),
        jnp.zeros((POOL * PAGE, width), jnp.bfloat16),
    )
    gathered = lax.all_gather(prefill_latent, "ctx", axis=0, tiled=True)
    attended = attend_blocks(initial[:3], prefill_query, gathered, 0)
    final = attended + (pick_rows(gathered, 0, source_rows, pool_live),)
    run_max, run_sum, weighted, pool_rows = final
    prefill_out = (weighted / run_sum[:, :, None]).astype(jnp.bfloat16)
    cache_dev = cache.shape[1]
    positions = device * cache_dev + jnp.arange(cache_dev, dtype=jnp.int32)
    resident_ok = (positions[None, :] < lengths[:, None])[:, None, :]
    resident_scores = (
        jnp.einsum("rhc,rtc->rht", decode_query, cache, preferred_element_type=jnp.float32) * SCALE
    )
    request_index = jnp.arange(REQ, dtype=jnp.int32)
    pool_ok = ((pool_request[None, :] == request_index[:, None]) & pool_live[None, :])[:, None, :]
    pool_scores = (
        jnp.einsum("rhc,kc->rhk", decode_query, pool_rows, preferred_element_type=jnp.float32)
        * SCALE
    )
    part_max = jnp.maximum(
        jnp.max(jnp.where(resident_ok, resident_scores, NEG), axis=2),
        jnp.max(jnp.where(pool_ok, pool_scores, NEG), axis=2),
    )
    resident_weights = jnp.where(resident_ok, jnp.exp(resident_scores - part_max[:, :, None]), 0.0)
    pool_weights = jnp.where(pool_ok, jnp.exp(pool_scores - part_max[:, :, None]), 0.0)
    part_sum = jnp.sum(resident_weights, axis=2) + jnp.sum(pool_weights, axis=2)
    part_out = jnp.einsum(
        "rht,rtv->rhv",
        resident_weights.astype(jnp.bfloat16),
        cache[:, :, :D_LAT],
        preferred_element_type=jnp.float32,
    )
    part_out = part_out + jnp.einsum(
        "rhk,kv->rhv",
        pool_weights.astype(jnp.bfloat16),
        pool_rows[:, :D_LAT],
        preferred_element_type=jnp.float32,
    )
    moved_max, moved_sum, moved_out = (
        lax.all_to_all(part_max[None], "ctx", split_axis=2, concat_axis=0, tiled=True),
        lax.all_to_all(part_sum[None], "ctx", split_axis=2, concat_axis=0, tiled=True),
        lax.all_to_all(part_out[None], "ctx", split_axis=2, concat_axis=0, tiled=True),
    )
    top_all = jnp.max(moved_max, axis=0)
    scales = jnp.exp(moved_max - top_all[None])
    own_sum = jnp.sum(moved_sum * scales, axis=0)
    own_out = jnp.sum(moved_out * scales[..., None], axis=0)
    decode_out = (own_out / own_sum[:, :, None]).astype(jnp.bfloat16)
    return (prefill_out, decode_out)


def solution(mesh):
    in_specs = (
        P("groups", "ctx", None),
        P(("groups", "ctx"), None),
        P("groups", None, None),
        P("groups", "ctx", None),
        P("groups"),
        P("groups", None),
    )
    out_specs = (P("groups", "ctx", None), P("groups", "ctx", None))
    return jax.shard_map(shards, mesh=mesh, in_specs=in_specs, out_specs=out_specs, check_vma=False)
```

profile of v0, /device:TPU:0, one launch (start us, length us, event | category | flops | bytes accessed | tf_op | source)
XLA Modules:
  0.0 114.0 jit_solution(10159602554596118152)
XLA Ops:
  7.2 0.7 all-gather.2.cloned.1.call-update
  7.9 0.7 slice_bitcast_fusion.2
  8.6 0.7 compare_bitcast_fusion
  9.3 0.1 select_reduce_fusion.4
  9.8 0.1 fusion.45
  10.4 0.7 broadcast_compare_fusion
  11.1 1.7 %select_reduce_fusion.2 = (f32[2,32]{1,0:T(2,128)S(1)}, f32[2,32,512]{2,1,0:T(8,128)S(1)}) fusion(pred[2,512]{1,0:T(4,128)(4,1)S(1)} %broadcast_compare_fusion, bf16[2,32,576]{2,1,0:T(8,128)(2,1)} %param.8, bf16[2,512,576]{1,2,0:T(8,128)(2,1)} %param.9), kind=kOutput, calls=%fused_computation.42 | convolution fusion | flops 37846976 | bytes 1385728 | tf_op jit(solution)/shard_map/rhc,rtc->rht/dot_general | solution.py:86
  12.8 55.0 %all-gather.2.cloned.1.call-done = bf16[1024,576]{1,0:T(8,128)(2,1)} async-done(((bf16[32,576]{1,0:T(8,128)(2,1)}), bf16[1024,576]{1,0:T(8,128)(2,1)}) %all-gather.2.cloned.1.call-update) | async-done | bytes 1179664 | tf_op jit(solution)/shard_map/all_gather | solution.py:77
  67.9 2.9 %gather_fusion = bf16[256,576]{1,0:T(8,128)(2,1)S(1)} fusion(bf16[1024,576]{1,0:T(8,128)(2,1)} %all-gather.2.cloned.1.call-done, s32[1024]{0:T(1024)S(1)} %pad_clamp_fusion), kind=kCustom, calls=%fused_computation | custom fusion | bytes 590848 | tf_op jit(solution)/shard_map/jit(_take)/gather | solution.py:51
  70.8 0.2 select_select_fusion
  70.9 0.3 select_reduce_fusion.3
  71.2 0.2 fusion.27
  71.5 0.2 fusion.35
  71.6 0.7 copy.21
  72.3 3.5 %all-to-all-start.1 = ((f32[1,2,32]{1,0,2:T(1,128)}), f32[1,2,32]{1,0,2:T(1,128)S(1)}, u32[]{:S(2)}, u32[]{:S(2)}) async-start(f32[1,2,32]{1,0,2:T(1,128)} %copy.21), calls=%async_computation.1 | async-start | bytes 32768 | tf_op jit(solution)/shard_map/all_to_all | solution.py:114
  75.8 0.2 fusion.29
  76.0 1.0 select_reduce_fusion.1
  77.0 1.0 select_reduce_fusion
  78.1 0.9 fusion
  79.0 0.8 fusion.12
  79.7 2.1 %fusion.4 = bf16[1024,1,512]{2,0,1:T(8,128)(2,1)} fusion(f32[1024,512]{1,0:T(8,128)S(1)} %fusion.12, f32[1024,512]{0,1:T(8,128)S(1)} %get-tuple-element.10, f32[1024]{0:T(1024)S(1)} %get-tuple-element.2, f32[1024]{0:T(1024)S(1)} %get-tuple-element.5, f32[1024]{0:T(1024)S(1)} %get-tuple-element.3, s32[512]{0:T(512)S(1)} %iota_add_fusion.2, ...), kind=kOutput, calls=%fused_computation.12 | convolution fusion | flops 542113792 | bytes 5785600 | tf_op jit(solution)/shard_map/ihj,jv->ihv/dot_general | solution.py:28
  81.9 0.7 copy.24
  82.5 0.5 all-to-all-done.1
  83.0 5.4 %all-to-all-start.2 = ((f32[1,2,32]{1,0,2:T(1,128)}), f32[1,2,32]{1,0,2:T(1,128)S(1)}, u32[]{:S(2)}, u32[]{:S(2)}) async-start(f32[1,2,32]{1,0,2:T(1,128)} %copy.24), calls=%async_computation.2 | async-start | bytes 32768 | tf_op jit(solution)/shard_map/all_to_all | solution.py:115
  88.4 1.6 %fusion.9 = f32[1,2,32,512]{3,2,1,0:T(8,128)S(1)} fusion(f32[2,32,512]{2,1,0:T(8,128)S(1)} %fusion.27, bf16[2,512,576]{1,2,0:T(8,128)(2,1)} %param.9, f32[2,32,512]{2,1,0:T(8,128)S(1)} %get-tuple-element.12, f32[2,32]{1,0:T(2,128)S(1)} %max.39, pred[2,512]{1,0:T(4,128)(4,1)S(1)} %broadcast_compare_fusion), kind=kOutput, calls=%fused_computation.18 | convolution fusion | flops 33685504 | bytes 1443072 | tf_op jit(solution)/shard_map/rht,rtv->rhv/dot_general | solution.py:101
  90.0 0.8 copy.20
  90.9 4.7 %all-to-all-done.2 = f32[1,2,32]{1,0,2:T(1,128)S(1)} async-done(((f32[1,2,32]{1,0,2:T(1,128)}), f32[1,2,32]{1,0,2:T(1,128)S(1)}, u32[]{:S(2)}, u32[]{:S(2)}) %all-to-all-start.2) | async-done | bytes 288 | tf_op jit(solution)/shard_map/all_to_all | solution.py:115
  95.6 2.6 %all-to-all-start = ((f32[1,2,32,512]{3,1,0,2:T(2,128)}), f32[1,2,32,512]{3,1,0,2:T(2,128)S(1)}, u32[]{:S(2)}, u32[]{:S(2)}) async-start(f32[1,2,32,512]{3,1,0,2:T(2,128)} %copy.20), calls=%async_computation | async-start | bytes 262144 | tf_op jit(solution)/shard_map/all_to_all | solution.py:116
  98.4 0.2 fusion.50
  98.6 7.8 %all-to-all-done = f32[1,2,32,512]{3,1,0,2:T(2,128)S(1)} async-done(((f32[1,2,32,512]{3,1,0,2:T(2,128)}), f32[1,2,32,512]{3,1,0,2:T(2,128)S(1)}, u32[]{:S(2)}, u32[]{:S(2)}) %all-to-all-start) | async-done | bytes 131104 | tf_op jit(solution)/shard_map/all_to_all | solution.py:116
  106.3 0.1 fusion.28
  106.5 0.7 fusion.47
  (34 shorter events, 1.2 us)
Async XLA Ops:
  7.2 68.8 %copy-start = (bf16[1024,1,576]{0,2,1:T(8,128)(2,1)S(1)}, bf16[1024,1,576]{0,2,1:T(8,128)(2,1)}, u32[]{:S(2)}) copy-start(bf16[1024,1,576]{0,2,1:T(8,128)(2,1)} %param.6) | copy-start | bytes 3538948
  7.2 60.7 %all-gather.2.cloned.1.call-start = ((), (), s32[]{:S(2)}) async-start(), calls=%async_computation.3 | async-start | bytes 1351680 | tf_op jit(solution)/shard_map/all_gather | solution.py:77
  12.8 58.1 %copy-start.2 = (bf16[2,32,576]{2,1,0:T(8,128)(2,1)S(1)}, bf16[2,32,576]{2,1,0:T(8,128)(2,1)}, u32[]{:S(2)}) copy-start(bf16[2,32,576]{2,1,0:T(8,128)(2,1)} %param.8) | copy-start | bytes 221188
  67.9 8.1 %copy-start.1 = (bf16[1024,576]{1,0:T(8,128)(2,1)S(1)}, bf16[1024,576]{1,0:T(8,128)(2,1)}, u32[]{:S(2)}) copy-start(bf16[1024,576]{1,0:T(8,128)(2,1)} %all-gather.2.cloned.1.call-done) | copy-start | bytes 3538948
  72.3 10.7 %all-to-all-start.1 = ((f32[1,2,32]{1,0,2:T(1,128)}), f32[1,2,32]{1,0,2:T(1,128)S(1)}, u32[]{:S(2)}, u32[]{:S(2)}) async-start(f32[1,2,32]{1,0,2:T(1,128)} %copy.21), calls=%async_computation.1 | async-start | bytes 32768 | tf_op jit(solution)/shard_map/all_to_all | solution.py:114
  83.0 12.6 %all-to-all-start.2 = ((f32[1,2,32]{1,0,2:T(1,128)}), f32[1,2,32]{1,0,2:T(1,128)S(1)}, u32[]{:S(2)}, u32[]{:S(2)}) async-start(f32[1,2,32]{1,0,2:T(1,128)} %copy.24), calls=%async_computation.2 | async-start | bytes 32768 | tf_op jit(solution)/shard_map/all_to_all | solution.py:115
  95.6 10.8 %all-to-all-start = ((f32[1,2,32,512]{3,1,0,2:T(2,128)}), f32[1,2,32,512]{3,1,0,2:T(2,128)S(1)}, u32[]{:S(2)}, u32[]{:S(2)}) async-start(f32[1,2,32,512]{3,1,0,2:T(2,128)} %copy.20), calls=%async_computation | async-start | bytes 262144 | tf_op jit(solution)/shard_map/all_to_all | solution.py:116
Sparse Core Ops, SparseCore 0:
  10.8 56.9 all-gather.1
where the time goes:
time: 114 us
  waiting for transfers between devices  68.6 us (60%)
  between operations  14.2 us (12%)
  starting transfers between devices  11.5 us (10%)
  matrix products  8.79 us (8%)
  local copies, waits for them, and re-layouts  6.53 us (6%)
  other arithmetic  4.38 us (4%)
    all_gather x1, waiting for transfers between devices, shards(): gathered = lax.all_gather(prefill_latent, 'ctx', axis=0, tiled=True)  55 us
    all_to_all x1, waiting for transfers between devices, shards(): lax.all_to_all(part_out[None], 'ctx', split_axis=2, concat_axis=0, tiled=...  7.77 us
    all_to_all x1, starting transfers between devices, shards(): lax.all_to_all(part_sum[None], 'ctx', split_axis=2, concat_axis=0, tiled=...  5.38 us
    all_to_all x1, waiting for transfers between devices, shards(): lax.all_to_all(part_sum[None], 'ctx', split_axis=2, concat_axis=0, tiled=...  4.65 us
    all_to_all x1, starting transfers between devices, shards(): lax.all_to_all(part_max[None], 'ctx', split_axis=2, concat_axis=0, tiled=...  3.48 us
    gather x1, local copies, waits for them, and re-layouts, pick_rows(): taken = jnp.take(shard_rows, jnp.clip(local_rows, 0, length - 1), axis=0)  2.89 us
    dot_general x2, matrix products, attend_block(): jnp.einsum('ihj,jv->ihv', weights.astype(jnp.bfloat16), shard_rows[:, :D_...  2.87 us
    all_to_all x1, starting transfers between devices, shards(): lax.all_to_all(part_out[None], 'ctx', split_axis=2, concat_axis=0, tiled=...  2.57 us
  transfers between devices with their start and end apart: 4, of which 4 were waited for; matrix products, arithmetic and copies ran while one was open for 13% of the time, Pallas kernels for 0%

commit v1 on v0

--- a/solution.py
+++ b/solution.py
@@ -112,7 +112,12 @@
     )
     moved_max, moved_sum, moved_out = (
         lax.all_to_all(part_max[None], "ctx", split_axis=2, concat_axis=0, tiled=True),
-        lax.all_to_all(part_sum[None], "ctx", split_axis=2, concat_axis=0, tiled=True),
+        jnp.concatenate(
+            lax.all_to_all(
+                jnp.stack(jnp.split(part_sum[None], lax.axis_size("ctx"), axis=2)), "ctx", 0, 0
+            ),
+            axis=0,
+        ),
         lax.all_to_all(part_out[None], "ctx", split_axis=2, concat_axis=0, tiled=True),
     )
     top_all = jnp.max(moved_max, axis=0)

time: 114 us -> 132 us (1.16)
  local copies, waits for them, and re-layouts: 6.53 us -> 24.2 us
    unnamed x6 -> x37, local copies, waits for them, and re-layouts: 0.02 us -> 16.9 us
  transfers between devices with their start and end apart: 4 -> 4, of which waited for: 4 -> 3; matrix products, arithmetic and copies ran while one was open for 13% -> 23% of each run, Pallas kernels for 0% -> 0%
where the time goes in v1:
time: 132 us
  waiting for transfers between devices  68.1 us (52%)
  local copies, waits for them, and re-layouts  24.2 us (18%)
  between operations  14.2 us (11%)
  starting transfers between devices  11.9 us (9%)
  matrix products  8.77 us (7%)
  other arithmetic  4.38 us (3%)
    all_gather x1, waiting for transfers between devices, shards(): gathered = lax.all_gather(prefill_latent, 'ctx', axis=0, tiled=True)  55 us
    unnamed x37, local copies, waits for them, and re-layouts  16.9 us
    all_to_all x1, waiting for transfers between devices, shards(): lax.all_to_all(part_out[None], 'ctx', split_axis=2, concat_axis=0, tiled=...  7.77 us
    all_to_all x1, starting transfers between devices, shards(): lax.all_to_all(jnp.stack(jnp.split(part_sum[None], lax.axis_size('ctx'),...  5.83 us
    all_to_all x1, waiting for transfers between devices, shards(): lax.all_to_all(jnp.stack(jnp.split(part_sum[None], lax.axis_size('ctx'),...  4.65 us
    all_to_all x1, starting transfers between devices, shards(): lax.all_to_all(part_max[None], 'ctx', split_axis=2, concat_axis=0, tiled=...  3.48 us
    gather x1, local copies, waits for them, and re-layouts, pick_rows(): taken = jnp.take(shard_rows, jnp.clip(local_rows, 0, length - 1), axis=0)  2.89 us
    dot_general x2, matrix products, attend_block(): jnp.einsum('ihj,jv->ihv', weights.astype(jnp.bfloat16), shard_rows[:, :D_...  2.86 us
  transfers between devices with their start and end apart: 4, of which 3 were waited for; matrix products, arithmetic and copies ran while one was open for 23% of the time, Pallas kernels for 0%

profile of v1, /device:TPU:0, one launch (start us, length us, event | category | flops | bytes accessed | tf_op | source)
XLA Modules:
  0.0 131.7 jit_solution(16980731557011177522)
XLA Ops:
  7.2 0.7 all-gather.2.cloned.1.call-update
  7.9 0.7 slice_bitcast_fusion.2
  8.6 0.7 compare_bitcast_fusion
  10.4 0.7 broadcast_compare_fusion
  11.1 1.7 %select_reduce_fusion.2 = (f32[2,32]{1,0:T(2,128)S(1)}, f32[2,32,512]{2,1,0:T(8,128)S(1)}) fusion(pred[2,512]{1,0:T(4,128)(4,1)S(1)} %broadcast_compare_fusion, bf16[2,32,576]{2,1,0:T(8,128)(2,1)} %param.8, bf16[2,512,576]{1,2,0:T(8,128)(2,1)} %param.9), kind=kOutput, calls=%fused_computation.42 | convolution fusion | flops 37846976 | bytes 1385728 | tf_op jit(solution)/shard_map/rhc,rtc->rht/dot_general | solution.py:86
  12.8 55.0 %all-gather.2.cloned.1.call-done = bf16[1024,576]{1,0:T(8,128)(2,1)} async-done(((bf16[32,576]{1,0:T(8,128)(2,1)}), bf16[1024,576]{1,0:T(8,128)(2,1)}) %all-gather.2.cloned.1.call-update) | async-done | bytes 1179664 | tf_op jit(solution)/shard_map/all_gather | solution.py:77
  67.9 2.9 %gather_fusion = bf16[256,576]{1,0:T(8,128)(2,1)S(1)} fusion(bf16[1024,576]{1,0:T(8,128)(2,1)} %all-gather.2.cloned.1.call-done, s32[1024]{0:T(1024)S(1)} %pad_clamp_fusion), kind=kCustom, calls=%fused_computation | custom fusion | bytes 590848 | tf_op jit(solution)/shard_map/jit(_take)/gather | solution.py:51
  73.3 0.7 copy.95
  74.0 3.5 %all-to-all-start.1 = ((f32[1,2,32]{1,0,2:T(1,128)}), f32[1,2,32]{1,0,2:T(1,128)S(1)}, u32[]{:S(2)}, u32[]{:S(2)}) async-start(f32[1,2,32]{1,0,2:T(1,128)} %copy.95), calls=%async_computation.1 | async-start | bytes 32768 | tf_op jit(solution)/shard_map/all_to_all | solution.py:114
  78.6 0.6 constant_dynamic-update-slice_fusion.28
  79.1 0.6 constant_dynamic-update-slice_fusion.27
  80.8 0.6 constant_dynamic-update-slice_fusion.24
  84.0 0.6 constant_dynamic-update-slice_fusion.18
  84.6 0.6 constant_dynamic-update-slice_fusion.17
  85.7 0.6 constant_dynamic-update-slice_fusion.15
  87.2 0.6 constant_dynamic-update-slice_fusion.12
  88.9 0.6 constant_dynamic-update-slice_fusion.9
  90.5 0.6 constant_dynamic-update-slice_fusion.6
  91.1 0.6 constant_dynamic-update-slice_fusion.5
  92.2 0.6 constant_dynamic-update-slice_fusion.3
  93.8 1.0 select_reduce_fusion.1
  94.8 1.0 select_reduce_fusion
  95.9 0.9 fusion
  96.8 0.8 fusion.12
  97.6 2.1 %fusion.4 = bf16[1024,1,512]{2,0,1:T(8,128)(2,1)} fusion(f32[1024,512]{1,0:T(8,128)S(1)} %fusion.12, f32[1024,512]{0,1:T(8,128)S(1)} %get-tuple-element.42, f32[1024]{0:T(1024)S(1)} %get-tuple-element.34, f32[1024]{0:T(1024)S(1)} %get-tuple-element.37, f32[1024]{0:T(1024)S(1)} %get-tuple-element.35, s32[512]{0:T(512)S(1)} %iota_add_fusion.2, ...), kind=kOutput, calls=%fused_computation.12 | convolution fusion | flops 542113792 | bytes 5785600 | tf_op jit(solution)/shard_map/ihj,jv->ihv/dot_general | solution.py:28
  100.2 5.8 %all-to-all-start.2 = ((f32[32,1,2,1]{2,3,1,0:T(1,128)}), f32[32,1,2,1]{2,3,1,0:T(1,128)S(1)}, u32[]{:S(2)}, u32[]{:S(2)}) async-start(f32[32,1,2,1]{2,3,1,0:T(1,128)} %constant_dynamic-update-slice_fusion), calls=%async_computation.2 | async-start | bytes 32768 | tf_op jit(solution)/shard_map/all_to_all | solution.py:116
  106.1 1.6 %fusion.9 = f32[1,2,32,512]{3,2,1,0:T(8,128)S(1)} fusion(f32[2,32,512]{2,1,0:T(8,128)S(1)} %fusion.27, bf16[2,512,576]{1,2,0:T(8,128)(2,1)} %param.9, f32[2,32,512]{2,1,0:T(8,128)S(1)} %get-tuple-element.44, f32[2,32]{1,0:T(2,128)S(1)} %max.39, pred[2,512]{1,0:T(4,128)(4,1)S(1)} %broadcast_compare_fusion), kind=kOutput, calls=%fused_computation.18 | convolution fusion | flops 33685504 | bytes 1443072 | tf_op jit(solution)/shard_map/rht,rtv->rhv/dot_general | solution.py:101
  107.7 0.8 copy.94
  108.6 4.7 %all-to-all-done.2 = f32[32,1,2,1]{2,3,1,0:T(1,128)S(1)} async-done(((f32[32,1,2,1]{2,3,1,0:T(1,128)}), f32[32,1,2,1]{2,3,1,0:T(1,128)S(1)}, u32[]{:S(2)}, u32[]{:S(2)}) %all-to-all-start.2) | async-done | bytes 288 | tf_op jit(solution)/shard_map/all_to_all | solution.py:116
  113.2 2.6 %all-to-all-start = ((f32[1,2,32,512]{3,1,0,2:T(2,128)}), f32[1,2,32,512]{3,1,0,2:T(2,128)S(1)}, u32[]{:S(2)}, u32[]{:S(2)}) async-start(f32[1,2,32,512]{3,1,0,2:T(2,128)} %copy.94), calls=%async_computation | async-start | bytes 262144 | tf_op jit(solution)/shard_map/all_to_all | solution.py:121
  116.3 7.8 %all-to-all-done = f32[1,2,32,512]{3,1,0,2:T(2,128)S(1)} async-done(((f32[1,2,32,512]{3,1,0,2:T(2,128)}), f32[1,2,32,512]{3,1,0,2:T(2,128)S(1)}, u32[]{:S(2)}, u32[]{:S(2)}) %all-to-all-start) | async-done | bytes 131104 | tf_op jit(solution)/shard_map/all_to_all | solution.py:121
  124.2 0.7 fusion.47
  (67 shorter events, 14.8 us)
Async XLA Ops:
  7.2 86.7 %copy-start = (bf16[1024,1,576]{0,2,1:T(8,128)(2,1)S(1)}, bf16[1024,1,576]{0,2,1:T(8,128)(2,1)}, u32[]{:S(2)}) copy-start(bf16[1024,1,576]{0,2,1:T(8,128)(2,1)} %param.6) | copy-start | bytes 3538948
  7.2 60.7 %all-gather.2.cloned.1.call-start = ((), (), s32[]{:S(2)}) async-start(), calls=%async_computation.3 | async-start | bytes 1351680 | tf_op jit(solution)/shard_map/all_gather | solution.py:77
  12.8 58.1 %copy-start.2 = (bf16[2,32,576]{2,1,0:T(8,128)(2,1)S(1)}, bf16[2,32,576]{2,1,0:T(8,128)(2,1)}, u32[]{:S(2)}) copy-start(bf16[2,32,576]{2,1,0:T(8,128)(2,1)} %param.8) | copy-start | bytes 221188
  67.9 26.0 %copy-start.1 = (bf16[1024,576]{1,0:T(8,128)(2,1)S(1)}, bf16[1024,576]{1,0:T(8,128)(2,1)}, u32[]{:S(2)}) copy-start(bf16[1024,576]{1,0:T(8,128)(2,1)} %all-gather.2.cloned.1.call-done) | copy-start | bytes 3538948
  74.0 26.3 %all-to-all-start.1 = ((f32[1,2,32]{1,0,2:T(1,128)}), f32[1,2,32]{1,0,2:T(1,128)S(1)}, u32[]{:S(2)}, u32[]{:S(2)}) async-start(f32[1,2,32]{1,0,2:T(1,128)} %copy.95), calls=%async_computation.1 | async-start | bytes 32768 | tf_op jit(solution)/shard_map/all_to_all | solution.py:114
  100.2 13.0 %all-to-all-start.2 = ((f32[32,1,2,1]{2,3,1,0:T(1,128)}), f32[32,1,2,1]{2,3,1,0:T(1,128)S(1)}, u32[]{:S(2)}, u32[]{:S(2)}) async-start(f32[32,1,2,1]{2,3,1,0:T(1,128)} %constant_dynamic-update-slice_fusion), calls=%async_computation.2 | async-start | bytes 32768 | tf_op jit(solution)/shard_map/all_to_all | solution.py:116
  113.2 10.8 %all-to-all-start = ((f32[1,2,32,512]{3,1,0,2:T(2,128)}), f32[1,2,32,512]{3,1,0,2:T(2,128)S(1)}, u32[]{:S(2)}, u32[]{:S(2)}) async-start(f32[1,2,32,512]{3,1,0,2:T(2,128)} %copy.94), calls=%async_computation | async-start | bytes 262144 | tf_op jit(solution)/shard_map/all_to_all | solution.py:121
Sparse Core Ops, SparseCore 0:
  10.8 56.9 all-gather.1
